TPU v7x, 32 devices: a whole 2x2x4 slice. The times are simulated.
32 devices in a mesh: dp: 8 (over z, x), tensor: 4 (over y, core).
Axes of the slice: x: 2, y: 2, z: 4, core: 2. Of those that a mesh axis runs over, the one named last changes fastest.
Arguments:
- cells_x: bfloat16 [16384, 768], P(('dp', 'tensor')), may hold values from -6 to 6
- cotangent: bfloat16 [16384, 768], P(('dp', 'tensor')), may hold values from -6 to 6
- gene_counts: int32 [8], replicated, may hold values from 300 to 2048, as said below
- slot_cell: int32 [8], P('dp'), may hold values from 0 to 7, each once
- norm_gain: bfloat16 [2, 768], replicated, may hold values from 0.5 to 1.5
- norm_shift: bfloat16 [2, 768], replicated, may hold values from -1 to 1
- out_bias: bfloat16 [2, 768], replicated, may hold values from -1 to 1
- w_qkv: bfloat16 [3, 768, 768], P(None, None, 'tensor'), may hold values from -0.3125 to 0.3125
- qv_bias: bfloat16 [2, 768], P(None, 'tensor'), may hold values from -1.5 to 1.5
- w_out: bfloat16 [768, 768], P('tensor'), may hold values from -1.75 to 1.75
- w_up: bfloat16 [768, 3072], P(None, 'tensor'), may hold values from -0.21875 to 0.21875
- up_bias: bfloat16 [3072], P('tensor'), may hold values from -1.5 to 1.5
- w_down: bfloat16 [3072, 768], P('tensor'), may hold values from -0.109375 to 0.109375
Outputs:
- block_out: bfloat16 [16384, 768], P(('dp', 'tensor'))
- input_grad: bfloat16 [16384, 768], P(('dp', 'tensor'))
- grad_norm_gain: float32 [2, 768], replicated
- grad_norm_shift: float32 [2, 768], replicated
- grad_out_bias: float32 [2, 768], replicated
- grad_qkv: float32 [3, 768, 768], P(None, None, 'tensor')
- grad_qv_bias: float32 [2, 768], P(None, 'tensor')
- grad_w_out: float32 [768, 768], P('tensor')
- grad_w_up: float32 [768, 3072], P(None, 'tensor')
- grad_up_bias: float32 [3072], P('tensor')
- grad_w_down: float32 [3072, 768], P('tensor')
Inputs may be any that keep to these rules, and one draw needn't show every extreme that they name: `gene_counts`: some cell has exactly 2048 expressed genes and some exactly 300. `slot_cell`: every cell is held in exactly one slot.
All inputs are finite; a program needn't handle non-finite values.
Results may differ from a plain program's by a relative error of at most 0.013.
The roundings to bfloat16 on the way count: a program that leaves them out, or rounds other values in their place, can miss the bound.
Values may be sent and summed in bfloat16 or wider, within the bound.
No kernel may reach another device: no remote copies, remote signals or barrier semaphores. Data moves between devices by JAX's collectives and lax.ppermute only.
A program may use at most 128 MiB of HBM per device.

v0:
```python
import jax
import jax.numpy as jnp
from jax import lax
from jax.sharding import PartitionSpec as P

HEAD_DIM = 64
SLOT = 2048
EPSILON = 1e-05
NEGATIVE = -1e30


def exact_gelu(hidden):
    return jax.nn.gelu(hidden, approximate=False)


def normalize(features, gain_row, shift_row):
    row_mean = jnp.mean(features, axis=-1, keepdims=True)
    centered = features - row_mean
    variance = jnp.mean(centered * centered, axis=-1, keepdims=True)
    inverse = lax.rsqrt(variance + EPSILON)
    scaled = centered * inverse
    return (scaled * gain_row.astype(jnp.float32) + shift_row.astype(jnp.float32), scaled, inverse)


def normalize_back(upstream, scaled, inverse, gain_row):
    graded = upstream * gain_row.astype(jnp.float32)
    grad_mean = jnp.mean(graded, axis=-1, keepdims=True)
    cross_mean = jnp.mean(graded * scaled, axis=-1, keepdims=True)
    return (
        inverse * (graded - grad_mean - scaled * cross_mean),
        jnp.sum(upstream * scaled, axis=0),
        jnp.sum(upstream, axis=0),
    )


def contract_last(left, right):
    return lax.dot_general(
        left, right, (((1,), (1,)), ((), ())), preferred_element_type=jnp.float32
    )


def contract_first(left, right):
    return lax.dot_general(
        left, right, (((0,), (0,)), ((), ())), preferred_element_type=jnp.float32
    )


def masked_scores(block_queries, key_heads, live_keys, score_scale):
    scores = (
        jnp.einsum("qhe,khe->hqk", block_queries, key_heads, preferred_element_type=jnp.float32)
        * score_scale
    )
    return jnp.where(live_keys[None, None, :], scores, NEGATIVE)


def attend_cell(query_heads, key_heads, value_heads, live_keys, block_rows):
    score_scale = query_heads.shape[-1] ** (-0.5)

    def one_block(block_index):
        block_queries = lax.dynamic_slice_in_dim(
            query_heads, block_index * block_rows, block_rows, 0
        )
        scores = masked_scores(block_queries, key_heads, live_keys, score_scale)
        row_max = jnp.max(scores, axis=-1, keepdims=True)
        exp_scores = jnp.exp(scores - row_max)
        row_total = jnp.sum(exp_scores, axis=-1, keepdims=True)
        soft_low = (exp_scores / row_total).astype(jnp.bfloat16)
        attended = jnp.einsum(
            "hqk,khe->qhe", soft_low, value_heads, preferred_element_type=jnp.float32
        )
        return (attended, (row_max + jnp.log(row_total))[..., 0])

    attended, log_totals = lax.map(one_block, jnp.arange(query_heads.shape[0] // block_rows))
    return (attended.reshape(query_heads.shape[0], -1), log_totals)


def attend_back(query_heads, key_heads, value_heads, grad_heads, log_totals, live_keys, block_rows):
    score_scale = query_heads.shape[-1] ** (-0.5)
    slot_rows = query_heads.shape[0]

    def one_block(sums_carry, block_index):
        key_sum, value_sum = sums_carry
        first_row = block_index * block_rows
        block_queries = lax.dynamic_slice_in_dim(query_heads, first_row, block_rows, 0)
        block_grads = lax.dynamic_slice_in_dim(grad_heads, first_row, block_rows, 0)
        scores = masked_scores(block_queries, key_heads, live_keys, score_scale)
        softmaxed = jnp.exp(scores - log_totals[block_index][..., None])
        soft_low = softmaxed.astype(jnp.bfloat16)
        prob_grad = jnp.einsum(
            "qhe,khe->hqk", block_grads, value_heads, preferred_element_type=jnp.float32
        )
        row_inner = jnp.sum(softmaxed * prob_grad, axis=-1, keepdims=True)
        score_grad = (score_scale * softmaxed * (prob_grad - row_inner)).astype(jnp.bfloat16)
        query_grad = jnp.einsum(
            "hqk,khe->qhe", score_grad, key_heads, preferred_element_type=jnp.float32
        )
        key_sum = key_sum + jnp.einsum(
            "hqk,qhe->khe", score_grad, block_queries, preferred_element_type=jnp.float32
        )
        value_sum = value_sum + jnp.einsum(
            "hqk,qhe->khe", soft_low, block_grads, preferred_element_type=jnp.float32
        )
        return ((key_sum, value_sum), query_grad)

    zero_heads = jnp.zeros(key_heads.shape, jnp.float32)
    (key_sum, value_sum), query_grad = lax.scan(
        one_block, (zero_heads, zero_heads), jnp.arange(slot_rows // block_rows)
    )
    return (
        query_grad.reshape(slot_rows, -1).astype(jnp.bfloat16),
        key_sum.reshape(slot_rows, -1).astype(jnp.bfloat16),
        value_sum.reshape(slot_rows, -1).astype(jnp.bfloat16),
    )


def per_device(
    cells_x,
    cotangent,
    gene_counts,
    slot_cell,
    norm_gain,
    norm_shift,
    out_bias,
    w_qkv,
    qv_bias,
    w_out,
    w_up,
    up_bias,
    w_down,
):
    row_count = cells_x.shape[0]
    cells_dev = slot_cell.shape[0]
    group_rows = cells_dev * SLOT
    block_rows = min(512, SLOT)
    cell_ids = jnp.arange(gene_counts.shape[0], dtype=jnp.int32)
    lengths = jnp.sum(
        jnp.where(slot_cell[:, None] == cell_ids[None, :], gene_counts[None, :], 0), axis=1
    )
    positions = jnp.arange(SLOT, dtype=jnp.int32)
    live_keys = positions[None, :] < lengths[:, None]
    row_index = lax.axis_index("tensor") * row_count + jnp.arange(row_count, dtype=jnp.int32)
    cell_of = row_index // SLOT
    length_of = jnp.sum(
        jnp.where(
            cell_of[:, None] == jnp.arange(cells_dev, dtype=jnp.int32)[None, :], lengths[None, :], 0
        ),
        axis=1,
    )
    live_rows = row_index % SLOT < length_of
    inputs = cells_x.astype(jnp.float32)
    normed_in, scaled_in, inverse_in = normalize(inputs, norm_gain[0], norm_shift[0])
    gathered_in = lax.all_gather(normed_in.astype(jnp.bfloat16), "tensor", axis=0, tiled=True)
    bias_rows = jnp.stack([qv_bias[0], jnp.zeros_like(qv_bias[0]), qv_bias[1]]).astype(jnp.float32)
    projected = jnp.einsum("rd,sdc->src", gathered_in, w_qkv, preferred_element_type=jnp.float32)
    projected = (projected + bias_rows[:, None, :]).astype(jnp.bfloat16)
    heads_local = projected.shape[2] // HEAD_DIM
    head_parts = projected.reshape(3, cells_dev, SLOT, heads_local, HEAD_DIM)
    attended, log_totals = lax.map(
        lambda packed: attend_cell(packed[0], packed[1], packed[2], packed[3], block_rows),
        (head_parts[0], head_parts[1], head_parts[2], live_keys),
    )
    attended_low = attended.reshape(group_rows, -1).astype(jnp.bfloat16)
    attn_sum = lax.psum_scatter(
        jnp.dot(attended_low, w_out, preferred_element_type=jnp.float32),
        "tensor",
        scatter_dimension=0,
        tiled=True,
    )
    middle = inputs + attn_sum + out_bias[0].astype(jnp.float32)
    normed_mid, scaled_mid, inverse_mid = normalize(middle, norm_gain[1], norm_shift[1])
    normed_mid_low = normed_mid.astype(jnp.bfloat16)
    up_full, bias_full, down_full = (w_up, up_bias, w_down)
    ffn_rows = lax.all_gather(normed_mid_low, "tensor", axis=0, tiled=True)
    hidden = jnp.dot(ffn_rows, up_full, preferred_element_type=jnp.float32) + bias_full.astype(
        jnp.float32
    )
    active, gelu_back = jax.vjp(exact_gelu, hidden)
    active_low = active.astype(jnp.bfloat16)
    branch = lax.psum_scatter(
        jnp.dot(active_low, w_down, preferred_element_type=jnp.float32).astype(jnp.bfloat16),
        "tensor",
        scatter_dimension=0,
        tiled=True,
    ).astype(jnp.float32)
    output = jnp.where(live_rows[:, None], middle + branch + out_bias[1].astype(jnp.float32), 0.0)
    block_out = output.astype(jnp.bfloat16)
    out_grad = jnp.where(live_rows[:, None], cotangent, jnp.zeros_like(cotangent))
    grad_rows = lax.all_gather(out_grad, "tensor", axis=0, tiled=True)
    hidden_grad = gelu_back(contract_last(grad_rows, down_full))[0].astype(jnp.bfloat16)
    down_grad = contract_first(active_low, grad_rows)
    up_grad = contract_first(ffn_rows, hidden_grad)
    up_bias_grad = jnp.sum(hidden_grad, axis=0, dtype=jnp.float32)
    mid_norm_grad = lax.psum_scatter(
        contract_last(hidden_grad, w_up), "tensor", scatter_dimension=0, tiled=True
    )
    mid_back, gain_mid, shift_mid = normalize_back(
        mid_norm_grad, scaled_mid, inverse_mid, norm_gain[1]
    )
    middle_grad = out_grad.astype(jnp.float32) + mid_back
    middle_rows = lax.all_gather(middle_grad.astype(jnp.bfloat16), "tensor", axis=0, tiled=True)
    attended_grad = contract_last(middle_rows, w_out).astype(jnp.bfloat16)
    out_weight_grad = contract_first(attended_low, middle_rows)
    grad_heads = attended_grad.reshape(cells_dev, SLOT, heads_local, HEAD_DIM)
    query_grad, key_grad, value_grad = lax.map(
        lambda packed: attend_back(
            packed[0], packed[1], packed[2], packed[3], packed[4], packed[5], block_rows
        ),
        (head_parts[0], head_parts[1], head_parts[2], grad_heads, log_totals, live_keys),
    )
    qkv_grad = jnp.stack([query_grad, key_grad, value_grad]).reshape(3, group_rows, -1)
    qkv_weight_grad = jnp.einsum(
        "src,rd->sdc", qkv_grad, gathered_in, preferred_element_type=jnp.float32
    )
    qv_bias_grad = jnp.stack(
        [
            jnp.sum(qkv_grad[0], axis=0, dtype=jnp.float32),
            jnp.sum(qkv_grad[2], axis=0, dtype=jnp.float32),
        ]
    )
    in_norm_grad = lax.psum_scatter(
        jnp.einsum("src,sdc->rd", qkv_grad, w_qkv, preferred_element_type=jnp.float32),
        "tensor",
        scatter_dimension=0,
        tiled=True,
    )
    in_back, gain_in, shift_in = normalize_back(in_norm_grad, scaled_in, inverse_in, norm_gain[0])
    input_grad = (middle_grad + in_back).astype(jnp.bfloat16)
    gain_grad, shift_grad, bias_grad = lax.psum(
        (
            jnp.stack([gain_in, gain_mid]),
            jnp.stack([shift_in, shift_mid]),
            jnp.stack([jnp.sum(middle_grad, axis=0), jnp.sum(out_grad, axis=0, dtype=jnp.float32)]),
        ),
        "tensor",
    )
    (
        qkv_weight_grad,
        qv_bias_grad,
        out_weight_grad,
        up_grad,
        up_bias_grad,
        down_grad,
        gain_grad,
        shift_grad,
        bias_grad,
    ) = lax.psum(
        (
            qkv_weight_grad,
            qv_bias_grad,
            out_weight_grad,
            up_grad,
            up_bias_grad,
            down_grad,
            gain_grad,
            shift_grad,
            bias_grad,
        ),
        "dp",
    )
    return (
        block_out,
        input_grad,
        gain_grad,
        shift_grad,
        bias_grad,
        qkv_weight_grad,
        qv_bias_grad,
        out_weight_grad,
        up_grad,
        up_bias_grad,
        down_grad,
    )


def solution(mesh):
    return jax.shard_map(
        per_device,
        mesh=mesh,
        in_specs=(
            P(("dp", "tensor"), None),
            P(("dp", "tensor"), None),
            P(),
            P("dp"),
            P(),
            P(),
            P(),
            P(None, None, "tensor"),
            P(None, "tensor"),
            P("tensor", None),
            P(None, "tensor"),
            P("tensor"),
            P("tensor", None),
        ),
        out_specs=(
            P(("dp", "tensor"), None),
            P(("dp", "tensor"), None),
            P(),
            P(),
            P(),
            P(None, None, "tensor"),
            P(None, "tensor"),
            P("tensor", None),
            P(None, "tensor"),
            P("tensor"),
            P("tensor", None),
        ),
        check_vma=False,
    )
```

profile of v0, /device:TPU:0, one launch (start us, length us, event | category | flops | bytes accessed | tf_op | source)
XLA Modules:
  0.0 833.0 jit_solution(6018540514751062280)
XLA Ops:
  15.0 29.9 %all-gather.5.cloned.1.call-done = bf16[2048,768]{1,0:T(8,128)(2,1)} async-done(((bf16[512,768]{1,0:T(8,128)(2,1)}), bf16[2048,768]{1,0:T(8,128)(2,1)}) %all-gather.5.cloned.1.call-update) | async-done | bytes 3145744 | tf_op jit(solution)/shard_map/all_gather | solution.py:152
  50.3 45.2 %while.48 = (s32[]{:T(128)}, bf16[4,512,3,64]{1,3,2,0:T(8,128)(2,1)}, f32[4,3,512]{2,1,0:T(4,128)}, s32[4]{0:T(128)S(1)}, bf16[2048,3,64]{0,2,1:T(8,128)(2,1)S(1...) while((s32[]{:T(128)}, ...), condition=%wide.region_6.7_spmd.clone, body=%wide.region_3.6_spmd.clone.sunk | while | flops 843055616 | bytes 46266624 | solution.py:73
  103.9 57.7 %reduce-scatter.5.cloned.1.call-done = f32[512,768]{1,0:T(8,128)} async-done(((f32[2048,768]{1,0:T(8,128)}), f32[512,768]{1,0:T(8,128)}) %reduce-scatter.5.cloned.1.call-update) | async-done | bytes 1572880 | tf_op jit(solution)/shard_map/reduce_scatter | solution.py:163
  170.4 23.4 %all-gather.7.cloned.1.call-done = bf16[2048,768]{1,0:T(8,128)(2,1)} async-done(((bf16[512,768]{1,0:T(8,128)(2,1)}), bf16[2048,768]{1,0:T(8,128)(2,1)}) %all-gather.7.cloned.1.call-update) | async-done | bytes 3145744 | tf_op jit(solution)/shard_map/all_gather | solution.py:173
  193.8 7.5 fusion.75
  201.3 23.0 %all-gather.9.cloned.1.call-done = bf16[2048,768]{1,0:T(8,128)(2,1)} async-done(((bf16[512,768]{1,0:T(8,128)(2,1)}), bf16[2048,768]{1,0:T(8,128)(2,1)}) %all-gather.9.cloned.1.call-update) | async-done | bytes 3145744 | tf_op jit(solution)/shard_map/all_gather | solution.py:188
  224.3 20.2 %convert_reduce_fusion = (f32[768]{0:T(1024)}, bf16[2048,768]{1,0:T(8,128)(2,1)S(1)}, f32[2048,768]{1,0:T(8,128)}) fusion(f32[2048,768]{1,0:T(8,128)} %fusion.75, f32[768]{0:T(1024)S(1)} %convert_element_type.147, bf16[2048,768]{1,0:T(8,128)(2,1)} %all-gather.9.cloned.1.call-done, bf16[768,768]{1,0:T(8,128)(2,1)S(1)} %copy-done), kind=kOutput, calls=%fused_computation.45 | convolution fusion | flops 2533883136 | bytes 20060160 | tf_op jit(solution)/shard_map/dot_general | solution.py:37
  262.1 47.7 %reduce-scatter.9.cloned.1.call-done = f32[512,768]{1,0:T(8,128)} async-done(((f32[2048,768]{1,0:T(8,128)}), f32[512,768]{1,0:T(8,128)}) %reduce-scatter.9.cloned.1.call-update) | async-done | bytes 1572880 | tf_op jit(solution)/shard_map/reduce_scatter | solution.py:193
  312.5 37.6 %reduce-scatter.7.cloned.1.call-done = bf16[512,768]{1,0:T(8,128)(2,1)} async-done(((bf16[2048,768]{1,0:T(8,128)(2,1)}), bf16[512,768]{1,0:T(8,128)(2,1)}) %reduce-scatter.7.cloned.1.call-update) | async-done | bytes 786448 | tf_op jit(solution)/shard_map/reduce_scatter | solution.py:179
  356.1 28.4 %all-gather.11.cloned.1.call-done = bf16[2048,768]{1,0:T(8,128)(2,1)} async-done(((bf16[512,768]{1,0:T(8,128)(2,1)}), bf16[2048,768]{1,0:T(8,128)(2,1)}) %all-gather.11.cloned.1.call-update) | async-done | bytes 3145744 | tf_op jit(solution)/shard_map/all_gather | solution.py:200
  389.4 122.9 %while.49 = (s32[]{:T(128)}, f32[2048,3,64]{0,2,1:T(8,128)S(1)}, f32[2048,3,64]{0,2,1:T(8,128)}, bf16[4,512,3,64]{1,3,2,0:T(8,128)(2,1)}, s32[4]{0:T(128)S(1)}, ...) while((s32[]{:T(128)}, f32[2048,3,64]{0,2,1:T(8,128)S(1)}, ...), condition=%wide.region_16.17_spmd.clone, body=%wide.region_14.16_spmd.clone.sunk | while | flops 2065170944 | bytes 129419576 | solution.py:106
  411.7 5.6 fusion.146
  426.8 5.5 fusion.145
  442.5 5.6 fusion.146
  457.7 5.5 fusion.145
  473.4 5.6 fusion.146
  488.6 5.5 fusion.145
  504.3 5.6 fusion.146
  516.6 6.0 convolution_bitcast_fusion.2
  522.7 7.1 fusion.78
  543.3 38.4 %reduce-scatter.11.cloned.1.call-done = f32[512,768]{1,0:T(8,128)} async-done(((f32[2048,768]{1,0:T(8,128)}), f32[512,768]{1,0:T(8,128)}) %reduce-scatter.11.cloned.1.call-update) | async-done | bytes 1572880 | tf_op jit(solution)/shard_map/reduce_scatter | solution.py:220
  583.9 10.2 %all-reduce.2 = (f32[2,768]{1,0:T(2,128)S(1)}, f32[2,768]{1,0:T(2,128)S(1)}, f32[2,768]{1,0:T(2,128)S(1)}) all-reduce(f32[2,768]{1,0:T(2,128)S(1)} %pad_maximum_fusion.1, f32[2,768]{1,0:T(2,128)S(1)} %pad_maximum_fusion.2, f32[2,768]{1,0:T(2,128)S(1)} %pad_maximum_fusion.3), channel_id=1, replica_groups=mesh['dp'=8,'tensor'=4] {'tensor'}, use_global_device_ids=true, to_apply=%region_22.23 | all-reduce | flops 4608 | bytes 36864 | tf_op jit(solution)/shard_map/psum | solution.py:228
  594.1 40.2 %all-reduce = (f32[2,768]{1,0:T(2,128)}, f32[2,768]{1,0:T(2,128)}, f32[2,768]{1,0:T(2,128)}, f32[2,192]{1,0:T(2,128)}, f32[768]{0:T(1024)}) all-reduce(f32[2,768]{1,0:T(2,128)S(1)} %get-tuple-element.288, f32[2,768]{1,0:T(2,128)S(1)} %get-tuple-element.289, ...), channel_id=1, replica_groups=mesh['dp'=8,'tensor'=4] {'dp'}, use_global_device_ids=true, to_apply=%region_23.24 | all-reduce | flops 5760 | bytes 46080 | tf_op jit(solution)/shard_map/psum | solution.py:246
  637.1 182.5 %all-reduce.5.cloned.1.call-done = (f32[3,768,192]{1,2,0:T(8,128)}, f32[192,768]{1,0:T(8,128)}, f32[768,768]{1,0:T(8,128)}, f32[768,768]{1,0:T(8,128)}) async-done(((f32[3,768,192]{1,2,0:T(8,128)}, f32[192,768]{1,0:T(8,128)}, f32[768,768]{1,0:T(8,128)}, f32[768,768]{1,0:T(8,128)}), (f32[3,768,192]{1,2,0:T(8,128)}, f32[192,768]{1,0:T(8,128)}, f32[768,768]{1,0:T(8,128)}, ...) | async-done | bytes 7077904 | tf_op jit(solution)/shard_map/psum | solution.py:246
  (253 shorter events, 206.3 us)
Async XLA Ops:
  7.2 217.1 %copy-start = (bf16[768,768]{1,0:T(8,128)(2,1)S(1)}, bf16[768,768]{1,0:T(8,128)(2,1)}, u32[]{:S(2)}) copy-start(bf16[768,768]{1,0:T(8,128)(2,1)} %param.29) | copy-start | bytes 3538948
  7.2 37.6 %copy-start.44 = (bf16[3,768,192]{1,2,0:T(8,128)(2,1)S(1)}, bf16[3,768,192]{1,2,0:T(8,128)(2,1)}, u32[]{:S(2)}) copy-start(bf16[3,768,192]{1,2,0:T(8,128)(2,1)} %param.24) | copy-start | bytes 2654212
  7.2 37.6 %all-gather.5.cloned.1.call-start = ((), (), s32[]{:S(2)}) async-start(), calls=%async_computation.4 | async-start | bytes 3932160 | tf_op jit(solution)/shard_map/all_gather | solution.py:152
  8.7 40.0 %copy-start.27 = (f32[512]{0:T(512)}, f32[512]{0:T(512)S(1)}, u32[]{:S(2)}) copy-start(f32[512]{0:T(512)S(1)} %broadcast_multiply_fusion.5) | copy-start | bytes 6148
  10.2 38.5 %copy-start.29 = (f32[512]{0:T(512)}, f32[512]{0:T(512)S(1)}, u32[]{:S(2)}) copy-start(f32[512]{0:T(512)S(1)} %add_rsqrt_fusion.1) | copy-start | bytes 6148
  11.1 37.7 %copy-start.25 = (f32[768]{0:T(1024)}, f32[768]{0:T(1024)S(1)}, u32[]{:S(2)}) copy-start(f32[768]{0:T(1024)S(1)} %get-tuple-element.312) | copy-start | bytes 9220
  13.5 148.2 %reduce-scatter.5.cloned.1.call-start = ((), (), s32[]{:S(2)}) async-start(), calls=%async_computation.5 | async-start | bytes 7864320 | tf_op jit(solution)/shard_map/reduce_scatter | solution.py:163
  102.7 91.1 %all-gather.7.cloned.1.call-start = ((), (), s32[]{:S(2)}) async-start(), calls=%async_computation.6 | async-start | bytes 3932160 | tf_op jit(solution)/shard_map/all_gather | solution.py:173
  165.1 59.2 %all-gather.9.cloned.1.call-start = ((), (), s32[]{:S(2)}) async-start(), calls=%async_computation.8 | async-start | bytes 3932160 | tf_op jit(solution)/shard_map/all_gather | solution.py:188
  169.2 140.6 %reduce-scatter.9.cloned.1.call-start = ((), (), s32[]{:S(2)}) async-start(), calls=%async_computation.9 | async-start | bytes 7864320 | tf_op jit(solution)/shard_map/reduce_scatter | solution.py:193
  250.8 99.3 %reduce-scatter.7.cloned.1.call-start = ((), (), s32[]{:S(2)}) async-start(), calls=%async_computation.7 | async-start | bytes 3932160 | tf_op jit(solution)/shard_map/reduce_scatter | solution.py:179
  262.0 88.1 %copy-start.11 = (bf16[512,768]{1,0:T(8,128)(2,1)S(1)}, bf16[512,768]{1,0:T(8,128)(2,1)}, u32[]{:S(2)}) copy-start(bf16[512,768]{1,0:T(8,128)(2,1)} %get-tuple-element.299) | copy-start | bytes 2359300
  262.0 88.1 %copy-start.31 = (f32[768]{0:T(1024)S(1)}, f32[768]{0:T(1024)}, u32[]{:S(2)}) copy-start(f32[768]{0:T(1024)} %get-tuple-element.235) | copy-start | bytes 9220
  262.0 88.1 %copy-start.40 = (pred[512]{0:T(512)(128)(4,1)S(1)}, pred[512]{0:T(512)(128)(4,1)}, u32[]{:S(2)}) copy-start(pred[512]{0:T(512)(128)(4,1)} %copy-done.39) | copy-start | bytes 1540
  262.1 122.5 %all-gather.11.cloned.1.call-start = ((), (), s32[]{:S(2)}) async-start(), calls=%async_computation.10 | async-start | bytes 3932160 | tf_op jit(solution)/shard_map/all_gather | solution.py:200
  355.9 225.8 %reduce-scatter.11.cloned.1.call-start = ((), (), s32[]{:S(2)}) async-start(), calls=%async_computation.11 | async-start | bytes 7864320 | tf_op jit(solution)/shard_map/reduce_scatter | solution.py:220
  356.1 33.3 %copy-start.4 = (bf16[2048,3,64]{0,2,1:T(8,128)(2,1)S(1)}, bf16[2048,3,64]{0,2,1:T(8,128)(2,1)}, u32[]{:S(2)}) copy-start(bf16[2048,3,64]{0,2,1:T(8,128)(2,1)} %copy-done.3) | copy-start | bytes 2359300
  522.6 297.0 %all-reduce.5.cloned.1.call-start = ((), (), s32[]{:S(2)}) async-start(), calls=%async_computation.12 | async-start | bytes 14155776 | tf_op jit(solution)/shard_map/psum | solution.py:246
  541.7 39.9 %copy-start.5 = (bf16[512,768]{1,0:T(8,128)(2,1)S(1)}, bf16[512,768]{1,0:T(8,128)(2,1)}, u32[]{:S(2)}) copy-start(bf16[512,768]{1,0:T(8,128)(2,1)} %param.17) | copy-start | bytes 2359300
  541.8 39.9 %copy-start.26 = (f32[768]{0:T(1024)S(1)}, f32[768]{0:T(1024)}, u32[]{:S(2)}) copy-start(f32[768]{0:T(1024)} %copy-done.25) | copy-start | bytes 9220
  541.8 39.9 %copy-start.28 = (f32[512]{0:T(512)S(1)}, f32[512]{0:T(512)}, u32[]{:S(2)}) copy-start(f32[512]{0:T(512)} %copy-done.27) | copy-start | bytes 6148
  541.8 39.9 %copy-start.30 = (f32[512]{0:T(512)S(1)}, f32[512]{0:T(512)}, u32[]{:S(2)}) copy-start(f32[512]{0:T(512)} %copy-done.29) | copy-start | bytes 6148
  541.8 52.3 %copy-start.38 = (f32[768]{0:T(1024)S(1)}, f32[768]{0:T(1024)}, u32[]{:S(2)}) copy-start(f32[768]{0:T(1024)} %get-tuple-element.291) | copy-start | bytes 9220
  541.8 92.5 %copy-start.8 = (f32[512,768]{1,0:T(8,128)S(1)}, f32[512,768]{1,0:T(8,128)}, u32[]{:S(2)}) copy-start(f32[512,768]{1,0:T(8,128)} %copy-done.7) | copy-start | bytes 4718596
  (41 other events, 179.4 us)
Sparse Core Ops, SparseCore 0:
  13.6 31.2 all-gather.4
  102.8 58.8 reduce-scatter.4
  165.2 28.4 all-gather.6
  195.7 28.4 all-gather.8
  251.0 58.8 reduce-scatter.8
  312.2 37.8 reduce-scatter.6
  356.0 28.4 all-gather.10
  522.7 58.8 reduce-scatter.10
  587.2 232.3 all-reduce.4
where the time goes:
time: 842 us; the launch traced here: 833 us
  waiting for transfers between devices  469 us (56%)
  matrix products  176 us (21%)
  other arithmetic  75.6 us (9%)
  blocking collectives  50.4 us (6%)
  local copies, waits for them, and re-layouts  33 us (4%)
  between operations  15.2 us (2%)
  loops' own time  12.7 us (2%)
    psum x1, waiting for transfers between devices, per_device(): lax.psum((qkv_weight_grad, qv_bias_grad, out_weight_grad, up_grad, up_bia...  182 us
    reduce_scatter x1, waiting for transfers between devices, per_device(): lax.psum_scatter(jnp.dot(attended_low, w_out, preferred_element_type=jnp....  57.7 us
    reduce_scatter x1, waiting for transfers between devices, per_device(): lax.psum_scatter(contract_last(hidden_grad, w_up), 'tensor', scatter_dime...  47.7 us
    psum x1, blocking collectives, per_device(): lax.psum((qkv_weight_grad, qv_bias_grad, out_weight_grad, up_grad, up_bia...  40.2 us
    reduce_scatter x1, waiting for transfers between devices, per_device(): lax.psum_scatter(jnp.einsum('src,sdc->rd', qkv_grad, w_qkv, preferred_ele...  38.4 us
    reduce_scatter x1, waiting for transfers between devices, per_device(): lax.psum_scatter(jnp.dot(active_low, w_down, preferred_element_type=jnp.f...  37.6 us
    all_gather x1, waiting for transfers between devices, per_device(): lax.all_gather(normed_in.astype(jnp.bfloat16), 'tensor', axis=0, tiled=True)  29.9 us
    dot_general x3, matrix products, contract_last(): lax.dot_general(left, right, (((1,), (1,)), ((), ())), preferred_element_...  28.7 us
  transfers between devices with their start and end apart: 9, of which 9 were waited for; matrix products, arithmetic and copies ran while one was open for 6% of the time, Pallas kernels for 0%

commit v1 on v0

--- a/solution.py
+++ b/solution.py
@@ -197,7 +197,25 @@
         mid_norm_grad, scaled_mid, inverse_mid, norm_gain[1]
     )
     middle_grad = out_grad.astype(jnp.float32) + mid_back
-    middle_rows = lax.all_gather(middle_grad.astype(jnp.bfloat16), "tensor", axis=0, tiled=True)
+    x = middle_grad.astype(jnp.bfloat16)
+    size, mine, width = (lax.axis_size("tensor"), lax.axis_index("tensor"), x.shape[0])
+    ahead = [(i, (i + 1) % size) for i in range(size)]
+    left_2 = [(i, (i - 1) % size) for i in range(size)]
+    whole = jnp.zeros((*x.shape[:0], size * width, *x.shape[0 + 1 :]), x.dtype)
+    whole = lax.dynamic_update_slice_in_dim(whole, x, mine * width, axis=0)
+    from_left = from_right = x
+    half = size // 2
+    for step in range(1, half + 1):
+        from_left = lax.ppermute(from_left, "tensor", ahead)
+        whole = lax.dynamic_update_slice_in_dim(
+            whole, from_left, (mine - step) % size * width, axis=0
+        )
+        if step < size - half:
+            from_right = lax.ppermute(from_right, "tensor", left_2)
+            whole = lax.dynamic_update_slice_in_dim(
+                whole, from_right, (mine + step) % size * width, axis=0
+            )
+    middle_rows = whole
     attended_grad = contract_last(middle_rows, w_out).astype(jnp.bfloat16)
     out_weight_grad = contract_first(attended_low, middle_rows)
     grad_heads = attended_grad.reshape(cells_dev, SLOT, heads_local, HEAD_DIM)

time: 842 us -> 849 us (level)
    all_gather x1 -> x0, waiting for transfers between devices: 28.4 us -> none  [per_device(): lax.all_gather(middle_grad.astype(jnp.bfloat16), 'tensor', axis=0, tiled=...]
    ppermute x0 -> x3, waiting for transfers between devices: none -> 26 us  [the longest x2 26 us: per_device(): from_left = lax.ppermute(from_left, 'tensor', ahead)]
    unnamed x93 -> x95, local copies, waits for them, and re-layouts: 17.2 us -> 17.6 us
  transfers between devices with their start and end apart: 9 -> 11, of which waited for: 9 -> 10; matrix products, arithmetic and copies ran while one was open for 6% -> 6% of each run, Pallas kernels for 0% -> 0%
where the time goes in v1:
time: 849 us; the launch traced here: 840 us
  waiting for transfers between devices  466 us (55%)
  matrix products  177 us (21%)
  other arithmetic  75.8 us (9%)
  blocking collectives  50.4 us (6%)
  local copies, waits for them, and re-layouts  38.9 us (5%)
  between operations  15.5 us (2%)
  loops' own time  13.8 us (2%)
    psum x1, waiting for transfers between devices, per_device(): lax.psum((qkv_weight_grad, qv_bias_grad, out_weight_grad, up_grad, up_bia...  182 us
    reduce_scatter x1, waiting for transfers between devices, per_device(): lax.psum_scatter(jnp.dot(attended_low, w_out, preferred_element_type=jnp....  57.7 us
    reduce_scatter x1, waiting for transfers between devices, per_device(): lax.psum_scatter(contract_last(hidden_grad, w_up), 'tensor', scatter_dime...  47.7 us
    psum x1, blocking collectives, per_device(): lax.psum((qkv_weight_grad, qv_bias_grad, out_weight_grad, up_grad, up_bia...  40.2 us
    reduce_scatter x1, waiting for transfers between devices, per_device(): lax.psum_scatter(jnp.einsum('src,sdc->rd', qkv_grad, w_qkv, preferred_ele...  38.2 us
    reduce_scatter x1, waiting for transfers between devices, per_device(): lax.psum_scatter(jnp.dot(active_low, w_down, preferred_element_type=jnp.f...  37.6 us
    all_gather x1, waiting for transfers between devices, per_device(): lax.all_gather(normed_in.astype(jnp.bfloat16), 'tensor', axis=0, tiled=True)  29.9 us
    dot_general x3, matrix products, contract_last(): lax.dot_general(left, right, (((1,), (1,)), ((), ())), preferred_element_...  28.8 us
  transfers between devices with their start and end apart: 11, of which 10 were waited for; matrix products, arithmetic and copies ran while one was open for 6% of the time, Pallas kernels for 0%

profile of v1, /device:TPU:0, one launch (start us, length us, event | category | flops | bytes accessed | tf_op | source)
XLA Modules:
  0.0 839.7 jit_solution(5775325854139061448)
XLA Ops:
  15.0 29.9 %all-gather.4.cloned.1.call-done = bf16[2048,768]{1,0:T(8,128)(2,1)} async-done(((bf16[512,768]{1,0:T(8,128)(2,1)}), bf16[2048,768]{1,0:T(8,128)(2,1)}) %all-gather.4.cloned.1.call-update) | async-done | bytes 3145744 | tf_op jit(solution)/shard_map/all_gather | solution.py:152
  50.3 45.2 %while.48 = (s32[]{:T(128)}, bf16[4,512,3,64]{1,3,2,0:T(8,128)(2,1)}, f32[4,3,512]{2,1,0:T(4,128)}, s32[4]{0:T(128)S(1)}, bf16[2048,3,64]{0,2,1:T(8,128)(2,1)S(1...) while((s32[]{:T(128)}, ...), condition=%wide.region_6.7_spmd.clone, body=%wide.region_3.6_spmd.clone.sunk | while | flops 843055616 | bytes 46266624 | solution.py:73
  103.9 57.7 %reduce-scatter.5.cloned.1.call-done = f32[512,768]{1,0:T(8,128)} async-done(((f32[2048,768]{1,0:T(8,128)}), f32[512,768]{1,0:T(8,128)}) %reduce-scatter.5.cloned.1.call-update) | async-done | bytes 1572880 | tf_op jit(solution)/shard_map/reduce_scatter | solution.py:163
  170.4 23.4 %all-gather.6.cloned.1.call-done = bf16[2048,768]{1,0:T(8,128)(2,1)} async-done(((bf16[512,768]{1,0:T(8,128)(2,1)}), bf16[2048,768]{1,0:T(8,128)(2,1)}) %all-gather.6.cloned.1.call-update) | async-done | bytes 3145744 | tf_op jit(solution)/shard_map/all_gather | solution.py:173
  193.8 7.5 fusion.75
  201.3 23.0 %all-gather.8.cloned.1.call-done = bf16[2048,768]{1,0:T(8,128)(2,1)} async-done(((bf16[512,768]{1,0:T(8,128)(2,1)}), bf16[2048,768]{1,0:T(8,128)(2,1)}) %all-gather.8.cloned.1.call-update) | async-done | bytes 3145744 | tf_op jit(solution)/shard_map/all_gather | solution.py:188
  224.3 20.2 %convert_reduce_fusion = (f32[768]{0:T(1024)}, bf16[2048,768]{1,0:T(8,128)(2,1)S(1)}, f32[2048,768]{1,0:T(8,128)}) fusion(f32[2048,768]{1,0:T(8,128)} %fusion.75, f32[768]{0:T(1024)S(1)} %convert_element_type.147, bf16[2048,768]{1,0:T(8,128)(2,1)} %all-gather.8.cloned.1.call-done, bf16[768,768]{1,0:T(8,128)(2,1)S(1)} %copy-done), kind=kOutput, calls=%fused_computation.45 | convolution fusion | flops 2533883136 | bytes 20060160 | tf_op jit(solution)/shard_map/dot_general | solution.py:37
  262.1 47.7 %reduce-scatter.9.cloned.1.call-done = f32[512,768]{1,0:T(8,128)} async-done(((f32[2048,768]{1,0:T(8,128)}), f32[512,768]{1,0:T(8,128)}) %reduce-scatter.9.cloned.1.call-update) | async-done | bytes 1572880 | tf_op jit(solution)/shard_map/reduce_scatter | solution.py:193
  312.5 37.6 %reduce-scatter.7.cloned.1.call-done = bf16[512,768]{1,0:T(8,128)(2,1)} async-done(((bf16[2048,768]{1,0:T(8,128)(2,1)}), bf16[512,768]{1,0:T(8,128)(2,1)}) %reduce-scatter.7.cloned.1.call-update) | async-done | bytes 786448 | tf_op jit(solution)/shard_map/reduce_scatter | solution.py:179
  358.5 17.7 %collective-permute-done = bf16[512,768]{1,0:T(8,128)(2,1)S(1)} collective-permute-done((bf16[512,768]{1,0:T(8,128)(2,1)}, bf16[512,768]{1,0:T(8,128)(2,1)S(1)}, u32[]{:S(2)}, u32[]{:S(2)}) %collective-permute-start) | collective-permute-done | bytes 786464 | tf_op jit(solution)/shard_map/ppermute | solution.py:209
  379.5 8.4 collective-permute-done.2
  394.9 124.2 %while.49 = (s32[]{:T(128)}, f32[2048,3,64]{0,2,1:T(8,128)S(1)}, f32[2048,3,64]{0,2,1:T(8,128)}, bf16[4,512,3,64]{1,3,2,0:T(8,128)(2,1)}, s32[4]{0:T(128)S(1)}, ...) while((s32[]{:T(128)}, f32[2048,3,64]{0,2,1:T(8,128)S(1)}, ...), condition=%wide.region_16.17_spmd.clone, body=%wide.region_14.16_spmd.clone.sunk | while | flops 2065170944 | bytes 129419576 | solution.py:106
  417.4 5.6 fusion.146
  432.9 5.5 fusion.145
  448.6 5.6 fusion.146
  464.1 5.5 fusion.145
  479.8 5.6 fusion.146
  511.0 5.6 fusion.146
  523.3 6.0 convolution_bitcast_fusion.2
  529.4 7.1 fusion.78
  549.9 38.2 %reduce-scatter.11.cloned.1.call-done = f32[512,768]{1,0:T(8,128)} async-done(((f32[2048,768]{1,0:T(8,128)}), f32[512,768]{1,0:T(8,128)}) %reduce-scatter.11.cloned.1.call-update) | async-done | bytes 1572880 | tf_op jit(solution)/shard_map/reduce_scatter | solution.py:238
  590.4 10.2 %all-reduce.2 = (f32[2,768]{1,0:T(2,128)S(1)}, f32[2,768]{1,0:T(2,128)S(1)}, f32[2,768]{1,0:T(2,128)S(1)}) all-reduce(f32[2,768]{1,0:T(2,128)S(1)} %pad_maximum_fusion.1, f32[2,768]{1,0:T(2,128)S(1)} %pad_maximum_fusion.2, f32[2,768]{1,0:T(2,128)S(1)} %pad_maximum_fusion.3), channel_id=1, replica_groups=mesh['dp'=8,'tensor'=4] {'tensor'}, use_global_device_ids=true, to_apply=%region_22.23 | all-reduce | flops 4608 | bytes 36864 | tf_op jit(solution)/shard_map/psum | solution.py:246
  600.7 40.2 %all-reduce = (f32[2,768]{1,0:T(2,128)}, f32[2,768]{1,0:T(2,128)}, f32[2,768]{1,0:T(2,128)}, f32[2,192]{1,0:T(2,128)}, f32[768]{0:T(1024)}) all-reduce(f32[2,768]{1,0:T(2,128)S(1)} %get-tuple-element.288, f32[2,768]{1,0:T(2,128)S(1)} %get-tuple-element.289, ...), channel_id=1, replica_groups=mesh['dp'=8,'tensor'=4] {'dp'}, use_global_device_ids=true, to_apply=%region_23.24 | all-reduce | flops 5760 | bytes 46080 | tf_op jit(solution)/shard_map/psum | solution.py:264
  643.7 182.3 %all-reduce.5.cloned.1.call-done = (f32[3,768,192]{1,2,0:T(8,128)}, f32[192,768]{1,0:T(8,128)}, f32[768,768]{1,0:T(8,128)}, f32[768,768]{1,0:T(8,128)}) async-done(((f32[3,768,192]{1,2,0:T(8,128)}, f32[192,768]{1,0:T(8,128)}, f32[768,768]{1,0:T(8,128)}, f32[768,768]{1,0:T(8,128)}), (f32[3,768,192]{1,2,0:T(8,128)}, f32[192,768]{1,0:T(8,128)}, f32[768,768]{1,0:T(8,128)}, ...) | async-done | bytes 7077904 | tf_op jit(solution)/shard_map/psum | solution.py:264
  (262 shorter events, 219.7 us)
Async XLA Ops:
  7.2 217.1 %copy-start = (bf16[768,768]{1,0:T(8,128)(2,1)S(1)}, bf16[768,768]{1,0:T(8,128)(2,1)}, u32[]{:S(2)}) copy-start(bf16[768,768]{1,0:T(8,128)(2,1)} %param.29) | copy-start | bytes 3538948
  7.2 37.6 %all-gather.4.cloned.1.call-start = ((), (), s32[]{:S(2)}) async-start(), calls=%async_computation.4 | async-start | bytes 3932160 | tf_op jit(solution)/shard_map/all_gather | solution.py:152
  8.7 40.0 %copy-start.28 = (f32[512]{0:T(512)}, f32[512]{0:T(512)S(1)}, u32[]{:S(2)}) copy-start(f32[512]{0:T(512)S(1)} %broadcast_multiply_fusion.5) | copy-start | bytes 6148
  10.2 38.5 %copy-start.30 = (f32[512]{0:T(512)}, f32[512]{0:T(512)S(1)}, u32[]{:S(2)}) copy-start(f32[512]{0:T(512)S(1)} %add_rsqrt_fusion.1) | copy-start | bytes 6148
  11.1 37.7 %copy-start.26 = (f32[768]{0:T(1024)}, f32[768]{0:T(1024)S(1)}, u32[]{:S(2)}) copy-start(f32[768]{0:T(1024)S(1)} %get-tuple-element.314) | copy-start | bytes 9220
  13.5 148.2 %reduce-scatter.5.cloned.1.call-start = ((), (), s32[]{:S(2)}) async-start(), calls=%async_computation.5 | async-start | bytes 7864320 | tf_op jit(solution)/shard_map/reduce_scatter | solution.py:163
  102.7 91.1 %all-gather.6.cloned.1.call-start = ((), (), s32[]{:S(2)}) async-start(), calls=%async_computation.6 | async-start | bytes 3932160 | tf_op jit(solution)/shard_map/all_gather | solution.py:173
  165.1 59.2 %all-gather.8.cloned.1.call-start = ((), (), s32[]{:S(2)}) async-start(), calls=%async_computation.8 | async-start | bytes 3932160 | tf_op jit(solution)/shard_map/all_gather | solution.py:188
  169.2 140.6 %reduce-scatter.9.cloned.1.call-start = ((), (), s32[]{:S(2)}) async-start(), calls=%async_computation.9 | async-start | bytes 7864320 | tf_op jit(solution)/shard_map/reduce_scatter | solution.py:193
  250.8 99.3 %reduce-scatter.7.cloned.1.call-start = ((), (), s32[]{:S(2)}) async-start(), calls=%async_computation.7 | async-start | bytes 3932160 | tf_op jit(solution)/shard_map/reduce_scatter | solution.py:179
  262.0 88.1 %copy-start.13 = (bf16[512,768]{1,0:T(8,128)(2,1)S(1)}, bf16[512,768]{1,0:T(8,128)(2,1)}, u32[]{:S(2)}) copy-start(bf16[512,768]{1,0:T(8,128)(2,1)} %get-tuple-element.299) | copy-start | bytes 2359300
  262.0 88.1 %copy-start.32 = (f32[768]{0:T(1024)S(1)}, f32[768]{0:T(1024)}, u32[]{:S(2)}) copy-start(f32[768]{0:T(1024)} %get-tuple-element.235) | copy-start | bytes 9220
  262.0 88.1 %copy-start.41 = (pred[512]{0:T(512)(128)(4,1)S(1)}, pred[512]{0:T(512)(128)(4,1)}, u32[]{:S(2)}) copy-start(pred[512]{0:T(512)(128)(4,1)} %copy-done.40) | copy-start | bytes 1540
  262.1 326.1 %reduce-scatter.11.cloned.1.call-start = ((), (), s32[]{:S(2)}) async-start(), calls=%async_computation.10 | async-start | bytes 7864320 | tf_op jit(solution)/shard_map/reduce_scatter | solution.py:238
  356.7 19.4 %collective-permute-start = (bf16[512,768]{1,0:T(8,128)(2,1)}, bf16[512,768]{1,0:T(8,128)(2,1)S(1)}, u32[]{:S(2)}, u32[]{:S(2)}) collective-permute-start(bf16[512,768]{1,0:T(8,128)(2,1)} %get-tuple-element.301), channel_id=1, source_target_pairs={{0,1},{1,2},{2,3},{3,0},{4,5},{5,6},{6,7},{7,4},{8,9},{9,10},{10,1... | collective-permute-start | bytes 2359304 | tf_op jit(solution)/shard_map/ppermute | solution.py:209
  356.7 20.6 %collective-permute-start.1 = (bf16[512,768]{1,0:T(8,128)(2,1)}, bf16[512,768]{1,0:T(8,128)(2,1)}, u32[]{:S(2)}, u32[]{:S(2)}) collective-permute-start(bf16[512,768]{1,0:T(8,128)(2,1)} %get-tuple-element.301), channel_id=1, source_target_pairs={{0,3},{1,0},{2,1},{3,2},{4,7},{5,4},{6,5},{7,6},{8,11},{9,8},{10,9... | collective-permute-start | bytes 2359304 | tf_op jit(solution)/shard_map/ppermute | solution.py:214
  376.1 11.7 %collective-permute-start.2 = (bf16[512,768]{1,0:T(8,128)(2,1)S(1)}, bf16[512,768]{1,0:T(8,128)(2,1)}, u32[]{:S(2)}, u32[]{:S(2)}) collective-permute-start(bf16[512,768]{1,0:T(8,128)(2,1)S(1)} %collective-permute-done), channel_id=1, source_target_pairs={{0,1},{1,2},{2,3},{3,0},{4,5},{5,6},{6,7},{7,4},{8,9},{9,10},{10,1... | collective-permute-start | bytes 2359304 | tf_op jit(solution)/shard_map/ppermute | solution.py:209
  529.4 296.7 %all-reduce.5.cloned.1.call-start = ((), (), s32[]{:S(2)}) async-start(), calls=%async_computation.11 | async-start | bytes 14155776 | tf_op jit(solution)/shard_map/psum | solution.py:264
  548.4 39.8 %copy-start.5 = (bf16[512,768]{1,0:T(8,128)(2,1)S(1)}, bf16[512,768]{1,0:T(8,128)(2,1)}, u32[]{:S(2)}) copy-start(bf16[512,768]{1,0:T(8,128)(2,1)} %param.17) | copy-start | bytes 2359300
  548.4 39.7 %copy-start.27 = (f32[768]{0:T(1024)S(1)}, f32[768]{0:T(1024)}, u32[]{:S(2)}) copy-start(f32[768]{0:T(1024)} %copy-done.26) | copy-start | bytes 9220
  548.4 39.7 %copy-start.29 = (f32[512]{0:T(512)S(1)}, f32[512]{0:T(512)}, u32[]{:S(2)}) copy-start(f32[512]{0:T(512)} %copy-done.28) | copy-start | bytes 6148
  548.4 39.7 %copy-start.31 = (f32[512]{0:T(512)S(1)}, f32[512]{0:T(512)}, u32[]{:S(2)}) copy-start(f32[512]{0:T(512)} %copy-done.30) | copy-start | bytes 6148
  548.5 52.2 %copy-start.39 = (f32[768]{0:T(1024)S(1)}, f32[768]{0:T(1024)}, u32[]{:S(2)}) copy-start(f32[768]{0:T(1024)} %get-tuple-element.291) | copy-start | bytes 9220
  548.5 92.4 %copy-start.8 = (f32[512,768]{1,0:T(8,128)S(1)}, f32[512,768]{1,0:T(8,128)}, u32[]{:S(2)}) copy-start(f32[512,768]{1,0:T(8,128)} %copy-done.7) | copy-start | bytes 4718596
  (44 other events, 228.7 us)
Sparse Core Ops, SparseCore 0:
  13.6 31.2 all-gather.3
  102.8 58.8 reduce-scatter.4
  165.2 28.4 all-gather.5
  195.7 28.4 all-gather.7
  251.0 58.8 reduce-scatter.8
  312.2 37.8 reduce-scatter.6
  529.5 58.6 reduce-scatter.10
  593.7 232.2 all-reduce.4
